TPU v7x, 256 devices: a whole 4x4x8 slice. The times are simulated.
256 devices in a mesh: group: 16 (over z, core), dev: 16 (over y, x).
Axes of the slice: x: 4, y: 4, z: 8, core: 2. Of those that a mesh axis runs over, the one named last changes fastest.
Arguments:
- tokens: bfloat16 [1024, 7168], P(('group', 'dev')), may hold values from -6 to 6
- group_ids: int32 [1024, 4], P(('group', 'dev')), may hold values from 0 to 15, as said below
- expert_ids: int32 [1024, 8], P(('group', 'dev')), may hold values from 0 to 63, as said below
- gate_scores: bfloat16 [1024, 8], P(('group', 'dev')), may hold values from 0.099609375 to 1
- w_gate: bfloat16 [7168, 65536], P(None, ('group', 'dev')), may hold values from -0.0625 to 0.0625
- w_up: bfloat16 [7168, 65536], P(None, ('group', 'dev')), may hold values from -0.0625 to 0.0625
- w_down: bfloat16 [65536, 7168], P(('group', 'dev')), may hold values from -0.1875 to 0.1875
Outputs:
- combined: bfloat16 [1024, 7168], P(('group', 'dev'))
Inputs may be any that keep to these rules, and one draw needn't show every extreme that they name: `group_ids`: each row names 4 different groups; among the 4 rows of one aligned block, at most 2 rows name any one group. `expert_ids`: each row names 8 different experts, exactly two in each group of the row's group_ids (expert x lies in group x // 4).
All inputs are finite; a program needn't handle non-finite values.
Results may differ from a plain program's by a relative error of at most 0.014.
Values may be sent and summed in bfloat16 or wider, within the bound.
No kernel may reach another device: no remote copies, remote signals or barrier semaphores. Data moves between devices by JAX's collectives and lax.ppermute only.
A program may use at most 64 MiB of HBM per device.

v0:
```python
import jax
import jax.numpy as jnp
from jax import lax
from jax.sharding import PartitionSpec as P

FF = 1024
EXP_GROUP = 4
CAP = 2


def local(tokens, group_ids, expert_ids, gate_scores, w_gate, w_up, w_down):
    group_count = lax.axis_size("group")
    dev_count = lax.axis_size("dev")
    model_width = tokens.shape[1]
    block_cols = w_gate.shape[1]
    expert_total = group_count * EXP_GROUP
    group_iota = jnp.arange(group_count, dtype=jnp.int32)
    member = jnp.sum((group_ids[:, :, None] == group_iota[None, None, :]).astype(jnp.int32), axis=1)
    before = jnp.cumsum(member, axis=0) - member
    slot_iota = jnp.arange(CAP, dtype=jnp.int32)
    select = (member.T[:, None, :] == 1) & (before.T[:, None, :] == slot_iota[None, :, None])
    select_rows = select.astype(jnp.bfloat16)
    matches = (
        expert_ids[:, :, None] == jnp.arange(expert_total, dtype=jnp.int32)[None, None, :]
    ).astype(jnp.float32)
    coef = jnp.sum(gate_scores.astype(jnp.float32)[:, :, None] * matches, axis=1)
    coef = coef.reshape(-1, group_count, EXP_GROUP).astype(jnp.bfloat16)
    send_rows = jnp.einsum(
        "gst,td->gsd", select_rows, tokens, preferred_element_type=jnp.float32
    ).astype(jnp.bfloat16)
    send_coef = jnp.einsum(
        "gst,tge->gse", select_rows, coef, preferred_element_type=jnp.float32
    ).astype(jnp.bfloat16)
    recv_rows, recv_coef = (
        lax.all_to_all(send_rows, "group", split_axis=0, concat_axis=0, tiled=True),
        lax.all_to_all(send_coef, "group", split_axis=0, concat_axis=0, tiled=True),
    )
    all_rows, all_coef = (
        lax.all_gather(recv_rows, "dev", axis=0, tiled=True),
        lax.all_gather(recv_coef, "dev", axis=0, tiled=True),
    )
    flat_rows = all_rows.reshape(-1, model_width)
    flat_coef = all_coef.reshape(-1, EXP_GROUP)
    dev_index = lax.axis_index("dev")
    owner_expert = (dev_index * block_cols + jnp.arange(block_cols, dtype=jnp.int32)) // FF
    onehot = (owner_expert[None, :] == jnp.arange(EXP_GROUP, dtype=jnp.int32)[:, None]).astype(
        jnp.bfloat16
    )
    gate_out = jnp.dot(flat_rows, w_gate, preferred_element_type=jnp.float32)
    up_out = jnp.dot(flat_rows, w_up, preferred_element_type=jnp.float32)
    col_scale = jnp.dot(flat_coef, onehot, preferred_element_type=jnp.float32)
    hidden = (col_scale * jax.nn.silu(gate_out) * up_out).astype(jnp.bfloat16)
    partial_value = lax.optimization_barrier(
        jnp.dot(hidden, w_down, preferred_element_type=jnp.float32).astype(jnp.bfloat16)
    )
    partial_value = partial_value.reshape(dev_count, group_count, CAP, model_width)
    moved_back = lax.all_to_all(partial_value, "group", split_axis=1, concat_axis=1, tiled=True)
    summed = lax.psum_scatter(
        moved_back.astype(jnp.float32).astype(jnp.bfloat16), "dev", scatter_dimension=0, tiled=True
    )
    returned = summed.reshape(group_count, CAP, model_width)
    combined = jnp.einsum("gst,gsd->td", select_rows, returned, preferred_element_type=jnp.float32)
    return combined.astype(jnp.bfloat16)


def solution(mesh):
    return jax.shard_map(
        local,
        mesh=mesh,
        in_specs=(
            P(("group", "dev"), None),
            P(("group", "dev"), None),
            P(("group", "dev"), None),
            P(("group", "dev"), None),
            P(None, ("group", "dev")),
            P(None, ("group", "dev")),
            P(("group", "dev"), None),
        ),
        out_specs=P(("group", "dev"), None),
        check_vma=False,
    )
```

profile of v0, /device:TPU:2, one launch (start us, length us, event | category | flops | bytes accessed | tf_op | source)
XLA Modules:
  0.0 424.0 jit_solution(7251178532512982187)
XLA Ops:
  6.5 0.8 convert_reduce_fusion
  7.4 0.4 convolution_convert_fusion.1
  7.8 0.5 copy.26
  8.2 23.2 %all_to_all.15 = bf16[16,2,7168]{2,1,0:T(2,128)(2,1)} all-to-all(bf16[16,2,7168]{2,1,0:T(2,128)(2,1)S(1)} %copy.26), channel_id=1, replica_groups=mesh['group'=16,'dev'=16] {'group'}, dimensions={0} | all-to-all | bytes 917504 | tf_op jit(solution)/shard_map/all_to_all | solution.py:35
  31.5 0.1 copy.24
  31.6 0.7 convert_element_type.33
  32.3 0.8 select_reduce_fusion
  33.1 0.1 convert_element_type.35
  33.2 0.8 convolution_convert_fusion.2
  33.9 4.0 all-to-all-start
  38.0 7.5 %all-to-all-done = bf16[16,2,4]{2,1,0:T(2,128)(2,1)S(1)} async-done(((bf16[16,2,4]{2,1,0:T(2,128)(2,1)}), bf16[16,2,4]{2,1,0:T(2,128)(2,1)S(1)}, u32[]{:S(2)}, u32[]{:S(2)}) %all-to-all-start) | async-done | bytes 288 | tf_op jit(solution)/shard_map/all_to_all | solution.py:36
  45.5 23.8 %all_gather.6 = bf16[256,2,4]{2,1,0:T(2,128)(2,1)S(1)} all-gather(bf16[16,2,4]{2,1,0:T(2,128)(2,1)S(1)} %all-to-all-done), channel_id=1, replica_groups=mesh['group'=16,'dev'=16] {'dev'}, dimensions={0}, use_global_device_ids=true | all-gather | bytes 4352 | tf_op jit(solution)/shard_map/all_gather | solution.py:40
  69.3 32.0 %all-gather.2.cloned.1.call-done = bf16[256,2,7168]{2,1,0:T(2,128)(2,1)} async-done(((bf16[16,2,7168]{2,1,0:T(2,128)(2,1)}), bf16[256,2,7168]{2,1,0:T(2,128)(2,1)}) %all-gather.2.cloned.1.call-update) | async-done | bytes 7340048 | tf_op jit(solution)/shard_map/all_gather | solution.py:39
  101.3 15.4 %reshape.40 = bf16[512,7168]{1,0:T(8,128)(2,1)} reshape(bf16[256,2,7168]{2,1,0:T(2,128)(2,1)} %all-gather.2.cloned.1.call-done) | data formatting | bytes 14680064 | tf_op jit(solution)/shard_map/reshape | solution.py:42
  116.7 6.3 %fusion.16 = f32[512,256]{1,0:T(8,128)S(1)} fusion(bf16[512,7168]{1,0:T(8,128)(2,1)} %reshape.40, bf16[7168,256]{1,0:T(8,128)(2,1)} %param.11), kind=kOutput, calls=%fused_computation.32 | convolution fusion | flops 1879048192 | bytes 11534336 | tf_op jit(solution)/shard_map/dot_general | solution.py:49
  123.1 0.9 copy-done.2
  124.0 2.1 fusion.17
  126.0 6.4 %convolution_convert_fusion = bf16[512,7168]{1,0:T(8,128)(2,1)} fusion(bf16[256,7168]{1,0:T(8,128)(2,1)} %param.13, f32[512,256]{1,0:T(8,128)S(1)} %fusion.17, bf16[512,4]{1,0:T(8,128)(2,1)S(1)} %bitcast.25, f32[512,256]{1,0:T(8,128)S(1)} %fusion.16, s32[256]{0:T(256)S(1)} %and_select_fusion), kind=kOutput, calls=%fused_computation | convolution fusion | flops 1884685312 | bytes 12063744 | tf_op jit(solution)/shard_map/dot_general | solution.py:54
  132.4 14.9 %reshape.41 = bf16[16,16,2,7168]{3,2,1,0:T(2,128)(2,1)} reshape(bf16[512,7168]{1,0:T(8,128)(2,1)} %convolution_convert_fusion) | data formatting | bytes 14680064 | tf_op jit(solution)/shard_map/reshape | solution.py:56
  147.3 6.6 %copy.27 = bf16[16,16,2,7168]{3,2,0,1:T(2,128)(2,1)S(1)} copy(bf16[16,16,2,7168]{3,2,1,0:T(2,128)(2,1)} %reshape.41) | data formatting | bytes 14680064 | tf_op jit(solution)/shard_map/reshape | solution.py:56
  153.9 168.9 %all_to_all.16 = bf16[16,16,2,7168]{3,2,0,1:T(2,128)(2,1)S(1)} all-to-all(bf16[16,16,2,7168]{3,2,0,1:T(2,128)(2,1)S(1)} %copy.27), channel_id=1, replica_groups=mesh['group'=16,'dev'=16] {'group'}, dimensions={1} | all-to-all | bytes 14680064 | tf_op jit(solution)/shard_map/all_to_all | solution.py:57
  322.8 7.0 %copy.28 = bf16[16,16,2,7168]{3,1,2,0:T(8,128)(2,1)} copy(bf16[16,16,2,7168]{3,2,0,1:T(2,128)(2,1)S(1)} %all_to_all.16) | data formatting | bytes 14680064 | tf_op jit(solution)/shard_map/all_to_all | solution.py:57
  329.8 85.4 %reduce-scatter.4.cloned.1.call-done = bf16[1,16,2,7168]{3,1,2,0:T(8,128)(2,1)} async-done(((bf16[16,16,2,7168]{3,1,2,0:T(8,128)(2,1)}), bf16[1,16,2,7168]{3,1,2,0:T(8,128)(2,1)}) %reduce-scatter.4.cloned.1.call-update) | async-done | bytes 458768
  415.2 1.9 fusion
  (14 shorter events, 0.2 us)
Async XLA Ops:
  6.5 0.9 copy-start
  6.5 94.7 %all-gather.2.cloned.1.call-start = ((), (), s32[]{:S(2)}) async-start(), calls=%async_computation.4 | async-start | bytes 7798784 | tf_op jit(solution)/shard_map/all_gather | solution.py:39
  33.9 11.5 %all-to-all-start = ((bf16[16,2,4]{2,1,0:T(2,128)(2,1)}), bf16[16,2,4]{2,1,0:T(2,128)(2,1)S(1)}, u32[]{:S(2)}, u32[]{:S(2)}) async-start(bf16[16,2,4]{2,1,0:T(2,128)(2,1)} %convolution_convert_fusion.2), calls=%async_computation | async-start | bytes 16384 | tf_op jit(solution)/shard_map/all_to_all | solution.py:36
  38.0 377.3 %reduce-scatter.4.cloned.1.call-start = ((), (), s32[]{:S(2)}) async-start(), calls=%async_computation.5 | async-start | bytes 7798784
  116.7 6.3 %copy-start.1 = (bf16[512,7168]{1,0:T(8,128)(2,1)S(1)}, bf16[512,7168]{1,0:T(8,128)(2,1)}, u32[]{:S(2)}) copy-start(bf16[512,7168]{1,0:T(8,128)(2,1)} %reshape.40) | copy-start | bytes 22020100
  116.7 7.3 %copy-start.2 = (bf16[7168,256]{1,0:T(8,128)(2,1)S(1)}, bf16[7168,256]{1,0:T(8,128)(2,1)}, u32[]{:S(2)}) copy-start(bf16[7168,256]{1,0:T(8,128)(2,1)} %param.12) | copy-start | bytes 11010052
Sparse Core Ops, SparseCore 0:
  31.6 69.5 all-gather.1
  330.0 85.2 reduce-scatter.3
where the time goes:
time: 425 us; the launch traced here: 424 us
  blocking collectives  216 us (51%)
  waiting for transfers between devices  125 us (29%)
  local copies, waits for them, and re-layouts  45.5 us (11%)
  matrix products  17.8 us (4%)
  between operations  13.5 us (3%)
    all_to_all x1, blocking collectives, local(): lax.all_to_all(partial_value, 'group', split_axis=1, concat_axis=1, tiled...  169 us
    unnamed x3, waiting for transfers between devices  85.4 us
    all_gather x1, waiting for transfers between devices, local(): lax.all_gather(recv_rows, 'dev', axis=0, tiled=True)  32 us
    all_gather x1, blocking collectives, local(): lax.all_gather(recv_coef, 'dev', axis=0, tiled=True)  23.8 us
    all_to_all x1, blocking collectives, local(): lax.all_to_all(send_rows, 'group', split_axis=0, concat_axis=0, tiled=True)  23.2 us
    reshape x2, local copies, waits for them, and re-layouts, local(): partial_value.reshape(dev_count, group_count, CAP, model_width)  21.5 us
    reshape x1, local copies, waits for them, and re-layouts, local(): flat_rows = all_rows.reshape(-1, model_width)  15.4 us
  transfers between devices with their start and end apart: 3, of which 3 were waited for; matrix products, arithmetic and copies ran while one was open for 1% of the time, Pallas kernels for 0%

commit v1 on v0

--- a/solution.py
+++ b/solution.py
@@ -36,10 +36,10 @@
         lax.all_to_all(send_coef, "group", split_axis=0, concat_axis=0, tiled=True),
     )
     all_rows, all_coef = (
-        lax.all_gather(recv_rows, "dev", axis=0, tiled=True),
+        lax.all_gather(recv_rows.reshape(-1, model_width), "dev", axis=0, tiled=True),
         lax.all_gather(recv_coef, "dev", axis=0, tiled=True),
     )
-    flat_rows = all_rows.reshape(-1, model_width)
+    flat_rows = all_rows
     flat_coef = all_coef.reshape(-1, EXP_GROUP)
     dev_index = lax.axis_index("dev")
     owner_expert = (dev_index * block_cols + jnp.arange(block_cols, dtype=jnp.int32)) // FF
@@ -53,12 +53,10 @@
     partial_value = lax.optimization_barrier(
         jnp.dot(hidden, w_down, preferred_element_type=jnp.float32).astype(jnp.bfloat16)
     )
-    partial_value = partial_value.reshape(dev_count, group_count, CAP, model_width)
-    moved_back = lax.all_to_all(partial_value, "group", split_axis=1, concat_axis=1, tiled=True)
-    summed = lax.psum_scatter(
-        moved_back.astype(jnp.float32).astype(jnp.bfloat16), "dev", scatter_dimension=0, tiled=True
+    summed = lax.psum_scatter(partial_value, "dev", scatter_dimension=0, tiled=True)
+    returned = lax.all_to_all(
+        summed.reshape(group_count, CAP, model_width), "group", split_axis=0, concat_axis=0, tiled=True
     )
-    returned = summed.reshape(group_count, CAP, model_width)
     combined = jnp.einsum("gst,gsd->td", select_rows, returned, preferred_element_type=jnp.float32)
     return combined.astype(jnp.bfloat16)
 

time: 425 us -> 240 us (0.56)
  blocking collectives: 216 us -> 68.5 us
  local copies, waits for them, and re-layouts: 45.5 us -> 3.73 us
    all_to_all x1, blocking collectives: 169 us -> 21.7 us  [local(): lax.all_to_all(summed.reshape(group_count, CAP, model_width), 'group', sp...]
    reduce_scatter x0 -> x1, waiting for transfers between devices: none -> 88.4 us  [local(): lax.psum_scatter(partial_value, 'dev', scatter_dimension=0, tiled=True)]
    unnamed x3 -> x2, waiting for transfers between devices: 85.4 us -> 0.03 us
    reshape x3 -> x2, local copies, waits for them, and re-layouts: 36.9 us -> 2.12 us  [the longest x1 1.19 us: local(): summed.reshape(group_count, CAP, model_width)]
    all_to_all x1 -> x0, local copies, waits for them, and re-layouts: 6.98 us -> none  [local(): lax.all_to_all(partial_value, 'group', split_axis=1, concat_axis=1, tiled...]
    dot_general x1, matrix products: 2.05 us -> 6.33 us  [local(): up_out = jnp.dot(flat_rows, w_up, preferred_element_type=jnp.float32)]
    dot_general x1, matrix products: 6.33 us -> 2.05 us  [local(): gate_out = jnp.dot(flat_rows, w_gate, preferred_element_type=jnp.float32)]
  transfers between devices with their start and end apart: 3 -> 3, of which waited for: 3 -> 3; matrix products, arithmetic and copies ran while one was open for 1% -> 0% of each run, Pallas kernels for 0% -> 0%
where the time goes in v1:
time: 240 us; the launch traced here: 237 us
  waiting for transfers between devices  129 us (54%)
  blocking collectives  68.5 us (29%)
  matrix products  16.8 us (7%)
  between operations  13.5 us (6%)
  starting transfers between devices  4.05 us (2%)
  local copies, waits for them, and re-layouts  3.73 us (2%)
    reduce_scatter x1, waiting for transfers between devices, local(): lax.psum_scatter(partial_value, 'dev', scatter_dimension=0, tiled=True)  88.4 us
    all_gather x1, waiting for transfers between devices, local(): lax.all_gather(recv_rows.reshape(-1, model_width), 'dev', axis=0, tiled=T...  33.4 us
    all_gather x1, blocking collectives, local(): lax.all_gather(recv_coef, 'dev', axis=0, tiled=True)  23.7 us
    all_to_all x1, blocking collectives, local(): lax.all_to_all(send_rows, 'group', split_axis=0, concat_axis=0, tiled=True)  23.1 us
    all_to_all x1, blocking collectives, local(): lax.all_to_all(summed.reshape(group_count, CAP, model_width), 'group', sp...  21.7 us
    all_to_all x1, waiting for transfers between devices, local(): lax.all_to_all(send_coef, 'group', split_axis=0, concat_axis=0, tiled=True)  7.46 us
    dot_general x1, matrix products, local(): jnp.dot(hidden, w_down, preferred_element_type=jnp.float32)  6.38 us
    dot_general x1, matrix products, local(): up_out = jnp.dot(flat_rows, w_up, preferred_element_type=jnp.float32)  6.33 us
  transfers between devices with their start and end apart: 3, of which 3 were waited for; matrix products, arithmetic and copies ran while one was open for 0% of the time, Pallas kernels for 0%

profile of v1, /device:TPU:2, one launch (start us, length us, event | category | flops | bytes accessed | tf_op | source)
XLA Modules:
  0.0 236.9 jit_solution(9839502086144225782)
XLA Ops:
  6.5 0.8 convert_reduce_fusion
  7.4 0.4 convolution_convert_fusion.1
  7.8 0.5 copy.20
  8.3 23.1 %all_to_all.15 = bf16[16,2,7168]{2,1,0:T(2,128)(2,1)S(1)} all-to-all(bf16[16,2,7168]{2,1,0:T(2,128)(2,1)S(1)} %copy.20), channel_id=1, replica_groups=mesh['group'=16,'dev'=16] {'group'}, dimensions={0} | all-to-all | bytes 917504 | tf_op jit(solution)/shard_map/all_to_all | solution.py:35
  31.4 0.9 reshape.37
  32.4 0.0 all-gather.2.cloned.1.call-update
  32.4 0.1 copy.18
  32.5 0.1 select_reduce_fusion
  32.6 0.1 convert_element_type.33
  32.7 0.8 convolution_convert_fusion.2
  33.5 4.0 %all-to-all-start = ((bf16[16,2,4]{2,1,0:T(2,128)(2,1)}), bf16[16,2,4]{2,1,0:T(2,128)(2,1)S(1)}, u32[]{:S(2)}, u32[]{:S(2)}) async-start(bf16[16,2,4]{2,1,0:T(2,128)(2,1)} %convolution_convert_fusion.2), calls=%async_computation | async-start | bytes 16384 | tf_op jit(solution)/shard_map/all_to_all | solution.py:36
  37.5 0.0 reduce-scatter.2.cloned.1.call-start
  37.6 7.5 %all-to-all-done = bf16[16,2,4]{2,1,0:T(2,128)(2,1)S(1)} async-done(((bf16[16,2,4]{2,1,0:T(2,128)(2,1)}), bf16[16,2,4]{2,1,0:T(2,128)(2,1)S(1)}, u32[]{:S(2)}, u32[]{:S(2)}) %all-to-all-start) | async-done | bytes 288 | tf_op jit(solution)/shard_map/all_to_all | solution.py:36
  45.0 23.7 %all_gather.6 = bf16[256,2,4]{2,1,0:T(2,128)(2,1)S(1)} all-gather(bf16[16,2,4]{2,1,0:T(2,128)(2,1)S(1)} %all-to-all-done), channel_id=1, replica_groups=mesh['group'=16,'dev'=16] {'dev'}, dimensions={0}, use_global_device_ids=true | all-gather | bytes 4352 | tf_op jit(solution)/shard_map/all_gather | solution.py:40
  68.8 33.4 %all-gather.2.cloned.1.call-done = bf16[512,7168]{1,0:T(8,128)(2,1)} async-done(((bf16[32,7168]{1,0:T(8,128)(2,1)}), bf16[512,7168]{1,0:T(8,128)(2,1)}) %all-gather.2.cloned.1.call-update) | async-done | bytes 7340048 | tf_op jit(solution)/shard_map/all_gather | solution.py:39
  102.2 6.3 %fusion.17 = f32[512,256]{1,0:T(8,128)S(1)} fusion(bf16[512,7168]{1,0:T(8,128)(2,1)} %all-gather.2.cloned.1.call-done, bf16[7168,256]{1,0:T(8,128)(2,1)} %param.12), kind=kOutput, calls=%fused_computation.33 | convolution fusion | flops 1879048192 | bytes 11534336 | tf_op jit(solution)/shard_map/dot_general | solution.py:50
  108.5 0.9 copy-done.4
  109.4 2.1 fusion.16
  111.5 6.4 %convolution_convert_fusion = bf16[512,7168]{1,0:T(8,128)(2,1)} fusion(bf16[256,7168]{1,0:T(8,128)(2,1)} %param.13, f32[512,256]{1,0:T(8,128)S(1)} %fusion.17, bf16[512,4]{1,0:T(8,128)(2,1)S(1)} %bitcast.21, f32[512,256]{1,0:T(8,128)S(1)} %fusion.16, s32[256]{0:T(256)S(1)} %and_select_fusion), kind=kOutput, calls=%fused_computation | convolution fusion | flops 1884685312 | bytes 12063744 | tf_op jit(solution)/shard_map/dot_general | solution.py:54
  117.9 0.0 reduce-scatter.2.cloned.1.call-update
  117.9 88.4 %reduce-scatter.2.cloned.1.call-done = bf16[32,7168]{1,0:T(8,128)(2,1)} async-done(((bf16[512,7168]{1,0:T(8,128)(2,1)}), bf16[32,7168]{1,0:T(8,128)(2,1)}) %reduce-scatter.2.cloned.1.call-update) | async-done | bytes 458768 | tf_op jit(solution)/shard_map/reduce_scatter | solution.py:56
  206.3 1.2 reshape.38
  207.5 21.7 %all_to_all.16 = bf16[16,2,7168]{2,1,0:T(2,128)(2,1)S(1)} all-to-all(bf16[16,2,7168]{2,1,0:T(2,128)(2,1)S(1)} %reshape.38), channel_id=1, replica_groups=mesh['group'=16,'dev'=16] {'group'}, dimensions={0} | all-to-all | bytes 917504 | tf_op jit(solution)/shard_map/all_to_all | solution.py:57
  229.2 0.9 fusion
  (16 shorter events, 0.1 us)
Async XLA Ops:
  6.5 0.9 copy-start
  6.5 26.0 %copy-start.2 = (bf16[4,8]{1,0:T(4,128)(2,1)S(1)}, bf16[4,8]{1,0:T(4,128)(2,1)}, u32[]{:S(2)}) copy-start(bf16[4,8]{1,0:T(4,128)(2,1)} %param.10) | copy-start | bytes 196
  6.5 26.0 %copy-start.1 = (s32[4,8]{1,0:T(4,128)S(1)}, s32[4,8]{1,0:T(4,128)}, u32[]{:S(2)}) copy-start(s32[4,8]{1,0:T(4,128)} %param.9) | copy-start | bytes 388
  6.5 95.6 %all-gather.2.cloned.1.call-start = ((), (), s32[]{:S(2)}) async-start(), calls=%async_computation.4 | async-start | bytes 7798784 | tf_op jit(solution)/shard_map/all_gather | solution.py:39
  33.5 11.5 %all-to-all-start = ((bf16[16,2,4]{2,1,0:T(2,128)(2,1)}), bf16[16,2,4]{2,1,0:T(2,128)(2,1)S(1)}, u32[]{:S(2)}, u32[]{:S(2)}) async-start(bf16[16,2,4]{2,1,0:T(2,128)(2,1)} %convolution_convert_fusion.2), calls=%async_computation | async-start | bytes 16384 | tf_op jit(solution)/shard_map/all_to_all | solution.py:36
  37.5 168.8 %reduce-scatter.2.cloned.1.call-start = ((), (), s32[]{:S(2)}) async-start(), calls=%async_computation.5 | async-start | bytes 7798784 | tf_op jit(solution)/shard_map/reduce_scatter | solution.py:56
  102.2 6.3 %copy-start.3 = (bf16[512,7168]{1,0:T(8,128)(2,1)S(1)}, bf16[512,7168]{1,0:T(8,128)(2,1)}, u32[]{:S(2)}) copy-start(bf16[512,7168]{1,0:T(8,128)(2,1)} %all-gather.2.cloned.1.call-done) | copy-start | bytes 22020100
  102.2 7.3 %copy-start.4 = (bf16[7168,256]{1,0:T(8,128)(2,1)S(1)}, bf16[7168,256]{1,0:T(8,128)(2,1)}, u32[]{:S(2)}) copy-start(bf16[7168,256]{1,0:T(8,128)(2,1)} %param.11) | copy-start | bytes 11010052
Sparse Core Ops, SparseCore 0:
  32.5 69.6 all-gather.1
  118.0 88.2 reduce-scatter.1
